TPU v7x, 32 devices: a whole 2x2x4 slice. The times are simulated.
32 devices in a mesh: chan: 4 (over y, x), space: 8 (over z, core).
Axes of the slice: x: 2, y: 2, z: 4, core: 2. Of those that a mesh axis runs over, the one named last changes fastest.
Arguments:
- volume: bfloat16 [32, 16, 256, 128], P('space', None, 'chan'), may hold values from -6 to 6
- kernel: bfloat16 [27, 256, 256], P(None, 'chan'), may hold values from -0.078125 to 0.078125
- bias: float32 [256], P('chan'), may hold values from -3 to 3
- cotangent: bfloat16 [32, 16, 256, 128], P('space', None, 'chan'), may hold values from -6 to 6
Outputs:
- output: bfloat16 [32, 16, 256, 128], P('space', None, 'chan')
- input_grad: bfloat16 [32, 16, 256, 128], P('space', None, 'chan')
- weight_grad: float32 [27, 256, 256], P(None, 'chan')
All inputs are finite; a program needn't handle non-finite values.
Results may differ from a plain program's by a relative error of at most 0.0049.
Values may be sent and summed in bfloat16 or wider, within the bound.
A program may use at most 128 MiB of HBM per device.

v0:
```python
import functools
import math

import jax
import jax.numpy as jnp
from jax import lax
from jax.experimental import pallas as pl
from jax.experimental.pallas import tpu as pltpu
from jax.sharding import PartitionSpec as P

F32 = jnp.float32
BF16 = jnp.bfloat16
VMEM_LIMIT = 60 * 1024 * 1024


def shifted(rows, amount):
    size_z = rows.shape[1]
    lane = lax.broadcasted_iota(jnp.int32, rows.shape, 1)
    edge = 0 if amount == 1 else size_z - 1
    return jnp.where(lane == edge, 0.0, pltpu.roll(rows, amount % size_z, 1))


class Gather:
    def __init__(self, source, planes, local_sem, send_sem, recv_sem, halo_send, halo_recv, peers):
        self.source, self.planes = source, planes
        self.local_sem, self.send_sem, self.recv_sem = local_sem, send_sem, recv_sem
        self.halo_send, self.halo_recv = halo_send, halo_recv
        self.size_x, self.size_y, self.part, self.size_z = source.shape
        self.peers = peers
        self.me = lax.axis_index("chan")
        self.slab = lax.axis_index("space")
        self.slabs = lax.axis_size("space")
        self.chans = self.part * peers
        self.has_lo, self.has_hi = self.slab > 0, self.slab < self.slabs - 1
        self.order = [1] + ([self.size_x] if self.size_x > 1 else []) + list(range(2, self.size_x))
        me = self.me
        if peers == 4:
            across = me // 2 * 2 + (1 - me % 2)
            along = (1 - me // 2) * 2 + me % 2
            self.owners = [me, across, along, 3 - me]
            self.near = [1, 2]
        else:
            self.owners = [(me + r) % peers for r in range(peers)]
            self.near = list(range(1, peers))

    def block(self, q, owner):
        rows = pl.ds(pl.multiple_of(q * self.chans + owner * self.part, self.part), self.part)
        return self.planes.at[rows, self.size_z : (self.size_y + 1) * self.size_z]

    def back(self, slot):
        return slot if self.peers == 4 else self.peers - slot

    def chan_copy(self, q, slot_held, toward, slot_there):
        return pltpu.make_async_remote_copy(
            src_ref=self.block(q, self.owners[slot_held]),
            dst_ref=self.block(q, self.owners[slot_held]),
            send_sem=self.send_sem.at[q, slot_there],
            recv_sem=self.recv_sem.at[q, slot_there],
            device_id=(self.me, self.slab) if toward is None else (self.owners[toward], self.slab),
            device_id_type=pl.DeviceIdType.MESH,
        )

    def arrived(self, q, slot):
        pltpu.make_async_remote_copy(
            src_ref=self.block(q, self.owners[slot]),
            dst_ref=self.block(q, self.owners[slot]),
            send_sem=self.send_sem.at[q, slot],
            recv_sem=self.recv_sem.at[q, slot],
            device_id=(self.owners[1], self.slab),
            device_id_type=pl.DeviceIdType.MESH,
        ).wait_recv()

    def halo_copy(self, slot, up):
        mine, theirs = (self.size_x, 0) if up else (1, self.size_x + 1)
        return pltpu.make_async_remote_copy(
            src_ref=self.block(mine, self.owners[slot]),
            dst_ref=self.block(theirs, self.owners[slot]),
            send_sem=self.halo_send.at[int(up), slot],
            recv_sem=self.halo_recv.at[int(up), slot],
            device_id=(self.me, self.slab + 1 if up else self.slab - 1),
            device_id_type=pl.DeviceIdType.MESH,
        )

    def halo_pass(self, q, slot):
        if q == self.size_x:

            @pl.when(self.has_hi)
            def _():
                self.halo_copy(slot, True).start()

        if q == 1:

            @pl.when(self.has_lo)
            def _():
                self.halo_copy(slot, False).start()

    def local_copy(self, q, y):
        rows = pl.ds(pl.multiple_of(q * self.chans + self.me * self.part, self.part), self.part)
        lanes = pl.ds(pl.multiple_of((y + 1) * self.size_z, self.size_z), self.size_z)
        return pltpu.make_async_copy(
            self.source.at[q - 1, y], self.planes.at[rows, lanes], self.local_sem.at[q]
        )

    def begin(self):
        for q in self.order:

            def put(y, _, q=q):
                self.local_copy(q, y).start()
                return 0

            lax.fori_loop(0, self.size_y, put, 0)
        barrier = pltpu.get_barrier_semaphore()
        for slot in range(1, self.peers):
            pl.semaphore_signal(
                barrier, inc=1, device_id=(self.owners[slot], self.slab), device_id_type=pl.DeviceIdType.MESH
            )
        for step in (1, self.slabs - 1):
            beside = (self.slab + step) % self.slabs
            pl.semaphore_signal(
                barrier, inc=1, device_id=(self.me, beside), device_id_type=pl.DeviceIdType.MESH
            )

        edge = jnp.zeros((self.planes.shape[0], self.size_z), BF16)
        self.planes[:, 0 : self.size_z] = edge
        self.planes[:, (self.size_y + 1) * self.size_z : (self.size_y + 2) * self.size_z] = edge
        cells = slice(self.size_z, (self.size_y + 1) * self.size_z)
        blank = jnp.zeros((self.chans, self.size_y * self.size_z), BF16)

        @pl.when(jnp.logical_not(self.has_lo))
        def _():
            self.planes[0 : self.chans, cells] = blank

        @pl.when(jnp.logical_not(self.has_hi))
        def _():
            self.planes[(self.size_x + 1) * self.chans : (self.size_x + 2) * self.chans, cells] = blank

        pl.semaphore_wait(barrier, self.peers + 1)

        for q in self.order:

            def done(y, _, q=q):
                self.local_copy(q, y).wait()
                return 0

            lax.fori_loop(0, self.size_y, done, 0)
        for stage in range(min(2, len(self.order))):
            self.send_own(stage)

    def send_own(self, stage):
        q = self.order[stage]
        for slot in self.near:
            self.chan_copy(q, 0, slot, self.back(slot)).start()
        self.halo_pass(q, 0)

    def relay(self, stage, q, slot):
        return self.peers == 4 and slot == (1 if stage % 2 else 2)

    def take_near(self, stage):
        q = self.order[stage]
        for slot in self.near:
            self.arrived(q, slot)
            if self.relay(stage, q, slot):
                self.chan_copy(q, slot, 3 - slot, 3).start()
            self.halo_pass(q, slot)
        if stage + 2 < len(self.order):
            self.send_own(stage + 2)

    def take_far(self, stage):
        q = self.order[stage]
        if self.peers == 4:
            self.arrived(q, 3)
            self.halo_pass(q, 3)

    def take_halo(self, up):
        @pl.when(self.has_lo if up else self.has_hi)
        def _():
            for slot in range(self.peers):
                mine, theirs = (self.size_x, 0) if up else (1, self.size_x + 1)
                pltpu.make_async_remote_copy(
                    src_ref=self.block(mine, self.owners[slot]),
                    dst_ref=self.block(theirs, self.owners[slot]),
                    send_sem=self.halo_send.at[int(up), slot],
                    recv_sem=self.halo_recv.at[int(up), slot],
                    device_id=(self.me, self.slab - 1 if up else self.slab + 1),
                    device_id_type=pl.DeviceIdType.MESH,
                ).wait_recv()

    def finish(self):
        for stage, q in enumerate(self.order):
            for slot in self.near:
                self.chan_copy(q, 0, slot, self.back(slot)).wait_send()
                if self.relay(stage, q, slot):
                    self.chan_copy(q, slot, 3 - slot, 3).wait_send()
        for up, there in ((True, self.has_hi), (False, self.has_lo)):

            @pl.when(there)
            def _(up=up):
                for slot in range(self.peers):
                    self.halo_copy(slot, up).wait_send()


def add_plane(planes, w_ref, acc, q, started, chans, size_y, size_z):
    size_x, rows, _ = acc.shape
    taps = [dx for dx in range(3) if 0 <= q - dx < size_x]
    first, last = taps[0], taps[-1] + 1
    count = 2

    def step(index, _):
        y = index * count
        total = None
        for dy in range(3):
            lanes = pl.ds(pl.multiple_of((y + dy) * size_z, size_z), count * size_z)
            part = jnp.dot(
                w_ref[first:last, dy].reshape((last - first) * rows, chans),
                planes[q * chans : (q + 1) * chans, lanes],
                preferred_element_type=F32,
            )
            total = part if total is None else total + part
        lanes = pl.ds(pl.multiple_of(y * size_z, size_z), count * size_z)
        for dx in taps:
            part = total[(dx - first) * rows : (dx - first + 1) * rows]
            if q - dx in started:
                acc[q - dx, :, lanes] += part
            else:
                acc[q - dx, :, lanes] = part
        return 0

    lax.fori_loop(0, size_y // count, step, 0)
    started.update(q - dx for dx in taps)


def tap_sum(acc, x, outs, lanes):
    return (
        acc[x, outs : 2 * outs, lanes]
        + shifted(acc[x, 0:outs, lanes], 1)
        + shifted(acc[x, 2 * outs : 3 * outs, lanes], -1)
    )


def conv(gather, w_ref, acc, finish_plane, aside):
    size_x, chans, size_y, size_z = gather.size_x, gather.chans, gather.size_y, gather.size_z
    started, count, left = set(), {x: 3 for x in range(size_x)}, list(aside)

    def plane(q):
        add_plane(gather.planes, w_ref, acc, q, started, chans, size_y, size_z)
        for dx in range(3):
            if q - dx in count:
                count[q - dx] -= 1
                if count[q - dx] == 0:
                    finish_plane(q - dx)

    gather.begin()
    stages = len(gather.order)
    for stage in range(stages):
        if left:
            left.pop(0)()
        gather.take_near(stage)
        if stage:
            gather.take_far(stage - 1)
            plane(gather.order[stage - 1])
    gather.take_halo(True)
    plane(0)
    gather.take_halo(False)
    plane(size_x + 1)
    gather.take_far(stages - 1)
    plane(gather.order[-1])
    gather.finish()


def forward_kernel(peers, vol_ref, w_ref, bias_ref, cot_ref, out_ref, grad_ref, sum_ref, planes, acc, three, *sems):
    gather = Gather(vol_ref, planes, *sems, peers)
    size_x, size_y, outs, size_z = cot_ref.shape

    def finish_plane(x):
        def step(y, _):
            lanes = pl.ds(pl.multiple_of(y * size_z, size_z), size_z)
            pre = tap_sum(acc, x, outs, lanes) + bias_ref[...]
            sig = jax.nn.sigmoid(pre)
            out_ref[x, y] = (pre * sig).astype(BF16)
            grad = cot_ref[x, y].astype(F32) * sig * (1.0 + pre * (1.0 - sig))
            held = grad.astype(BF16)
            grad_ref[x, y] = held
            grad = held.astype(F32)
            three[x, 0:outs, lanes] = shifted(grad, -1).astype(BF16)
            three[x, outs : 2 * outs, lanes] = held
            three[x, 2 * outs : 3 * outs, lanes] = shifted(grad, 1).astype(BF16)
            return 0

        lax.fori_loop(0, size_y, step, 0)

    conv(gather, w_ref, acc, finish_plane, ())
    sum_ref[...] = jnp.zeros_like(sum_ref)
    chans, cells = gather.chans, size_y * size_z

    def step(x, _):
        for dy in range(3):
            cube = planes[pl.ds(pl.multiple_of(x * chans, chans), 3 * chans), dy * size_z : dy * size_z + cells]
            part = lax.dot_general(
                three[x], cube, (((1,), (1,)), ((), ())), preferred_element_type=F32
            )
            for dx in range(3):
                sum_ref[dx, dy] += part[:, dx * chans : (dx + 1) * chans]
        return 0

    lax.fori_loop(0, size_x, step, 0)
    sum_ref[...] = sum_ref[...] * (1.0 / math.sqrt(size_x * cells * gather.slabs))


def input_kernel(peers, grad_ref, pieces_ref, out_ref, planes, acc, w_ref, *sems):
    gather = Gather(grad_ref, planes, *sems, peers)
    size_x, size_y, outs, size_z = out_ref.shape

    def turn():
        def step(tap, _):
            dx, dy, dz = tap // 9, tap // 3 % 3, tap % 3
            whole = jnp.concatenate([pieces_ref[i, 26 - tap] for i in range(peers)], axis=0)
            rows = pl.ds(pl.multiple_of(dz * outs, outs), outs)
            w_ref[dx, dy, rows] = whole.astype(F32).T.astype(BF16)
            return 0

        lax.fori_loop(0, 27, step, 0)

    def finish_plane(x):
        def step(y, _):
            lanes = pl.ds(pl.multiple_of(y * size_z, size_z), size_z)
            out_ref[x, y] = tap_sum(acc, x, outs, lanes).astype(BF16)
            return 0

        lax.fori_loop(0, size_y, step, 0)

    conv(gather, w_ref, acc, finish_plane, (turn,))


def call(kernel, args, outs, extra, rows, flops, identity):
    whole = pl.BlockSpec(memory_space=pltpu.VMEM)
    peers = lax.axis_size("chan")
    size_x, size_y, part, size_z = args[0].shape
    planes = size_x + 2
    size = sum(a.size * a.dtype.itemsize for a in args)
    return pl.pallas_call(
        functools.partial(kernel, peers),
        out_shape=outs,
        in_specs=[pl.BlockSpec(memory_space=pl.ANY)] + [whole] * (len(args) - 1),
        out_specs=jax.tree.map(lambda _: whole, outs),
        scratch_shapes=[
            pltpu.VMEM((planes * part * peers, (size_y + 2) * size_z), BF16),
            pltpu.VMEM((size_x, rows, size_y * size_z), F32),
            *extra,
            pltpu.SemaphoreType.DMA((planes,)),
            pltpu.SemaphoreType.DMA((planes, peers)),
            pltpu.SemaphoreType.DMA((planes, peers)),
            pltpu.SemaphoreType.DMA((2, peers)),
            pltpu.SemaphoreType.DMA((2, peers)),
        ],
        compiler_params=pltpu.CompilerParams(
            vmem_limit_bytes=VMEM_LIMIT, collective_id=identity, has_side_effects=True
        ),
        cost_estimate=pl.CostEstimate(flops=flops, bytes_accessed=size, transcendentals=0),
    )(*args)


def on_device(volume, kernel, bias, cotangent):
    size_x, size_y, chans_local, size_z = volume.shape
    taps, outs, chans = kernel.shape
    shape = jax.ShapeDtypeStruct
    flops = 2 * size_x * size_y * size_z * taps * outs * chans
    w_forward = kernel.reshape(3, 3, 3 * outs, chans)
    peers = lax.axis_size("chan")
    ins, all_outs = chans // peers, outs * peers
    pieces = kernel.reshape(taps, outs, peers, ins).transpose(2, 0, 1, 3)
    pieces = lax.all_to_all(pieces, "chan", split_axis=0, concat_axis=0, tiled=True)
    column = jnp.broadcast_to(bias.reshape(outs, 1), (outs, size_z))

    output, grad_pre, partial = call(
        forward_kernel,
        (volume, w_forward, column, cotangent),
        (
            shape(cotangent.shape, BF16),
            shape(cotangent.shape, BF16),
            shape((3, 3, 3 * outs, chans), F32),
        ),
        [pltpu.VMEM((size_x, 3 * outs, size_y * size_z), BF16)],
        3 * outs,
        2 * flops,
        0,
    )
    weight_grad = lax.psum(partial, "space").reshape(taps, outs, chans)
    input_grad = call(
        input_kernel,
        (grad_pre, pieces),
        shape(volume.shape, BF16),
        [pltpu.VMEM((3, 3, 3 * ins, all_outs), BF16)],
        3 * ins,
        flops,
        1,
    )
    return output, input_grad, weight_grad


def solution(mesh):
    return jax.shard_map(
        on_device,
        mesh=mesh,
        in_specs=(
            P("space", None, "chan", None),
            P(None, "chan", None),
            P("chan"),
            P("space", None, "chan", None),
        ),
        out_specs=(
            P("space", None, "chan", None),
            P("space", None, "chan", None),
            P(None, "chan", None),
        ),
        check_vma=False,
    )
```

profile of v0, /device:TPU:0, one launch (start us, length us, event | category | flops | bytes accessed | tf_op | source)
XLA Modules:
  0.0 177.3 jit_solution(12326371878960706362)
XLA Ops:
  7.2 3.0 %reshape.18 = bf16[27,64,4,64]{3,2,1,0:T(4,128)(2,1)S(1)} reshape(bf16[27,64,256]{2,1,0:T(8,128)(2,1)} %param.5) | data formatting | bytes 1769472 | tf_op jit(solution)/shard_map/reshape | solution.py:370
  10.1 0.4 copy.9
  10.6 0.0 copy-start.3
  10.6 2.5 %reshape.20 = bf16[4,2,55296]{2,1,0:T(2,128)(2,1)} reshape(bf16[4,27,64,64]{3,2,1,0:T(8,128)(2,1)S(1)} %bitcast.5) | data formatting | bytes 1769472
  13.1 5.2 %all-to-all-start = ((bf16[4,2,55296]{2,1,0:T(2,128)(2,1)}), bf16[4,2,55296]{2,1,0:T(2,128)(2,1)S(1)}, u32[]{:S(2)}, u32[]{:S(2)}) async-start(bf16[4,2,55296]{2,1,0:T(2,128)(2,1)} %reshape.20), calls=%async_computation | async-start | bytes 1769472 | tf_op jit(solution)/shard_map/all_to_all | solution.py:371
  18.3 0.0 all-reduce.2.cloned.1.call-start
  18.3 0.0 copy-done.3
  18.3 0.7 broadcast_in_dim.2.bias_ref
  19.0 81.6 %shard_map.67 = (bf16[4,16,64,128]{3,2,1,0:T(8,128)(2,1)}, bf16[4,16,64,128]{3,2,1,0:T(8,128)(2,1)}, f32[3,3,192,256]{3,2,1,0:T(8,128)}) custom-call(bf16[4,16,64,128]{3,2,1,0:T(8,128)(2,1)} %vol_ref.1, bf16[3,3,192,256]{3,2,1,0:T(8,128)(2,1)} %bitcast.7, f32[64,128]{1,0:T(8,128)} %broadcast_in_dim.2.bias_ref, bf16[4,16,64,128]{3,2,1,0:T(8,128)(2,1)} %cot_ref.1), custom_call_target="tpu_custom_call" | custom-call | flops 14495514624 | bytes 3014656 | tf_op jit(solution)/shard_map/pallas_call | solution.py:340
  100.6 0.0 all-reduce.2.cloned.1.call-update
  100.6 0.0 all-to-all-done
  100.6 2.5 %reshape.21.pieces_ref = bf16[4,27,64,64]{3,2,1,0:T(8,128)(2,1)} reshape(bf16[4,2,55296]{2,1,0:T(2,128)(2,1)S(1)} %all-to-all-done) | data formatting | bytes 1769472
  103.1 0.0 copy-start.1
  103.2 56.9 %shard_map.68 = bf16[4,16,64,128]{3,2,1,0:T(8,128)(2,1)} custom-call(bf16[4,16,64,128]{3,2,1,0:T(8,128)(2,1)} %get-tuple-element.7.grad_ref, bf16[4,27,64,64]{3,2,1,0:T(8,128)(2,1)} %reshape.21.pieces_ref), custom_call_target="tpu_custom_call" | custom-call | flops 7247757312 | bytes 1933312 | tf_op jit(solution)/shard_map/pallas_call | solution.py:340
  160.1 0.0 copy-start.2
  160.1 7.2 %all-reduce.2.cloned.1.call-done = f32[27,64,256]{2,1,0:T(8,128)} async-done(((f32[27,64,256]{2,1,0:T(8,128)}), f32[27,64,256]{2,1,0:T(8,128)}) %all-reduce.2.cloned.1.call-update) | async-done | bytes 1769488 | tf_op jit(solution)/shard_map/psum | solution.py:387
  167.3 0.0 copy-done.1
  167.3 0.0 copy-start
  167.3 1.0 copy.14
  168.3 0.0 copy-done.2
  168.3 1.0 copy.15
  169.3 0.0 copy-done
  169.3 1.2 copy.16
Async XLA Ops:
  10.6 7.7 %copy-start.3 = (f32[64]{0:T(128)S(1)}, f32[64]{0:T(128)}, u32[]{:S(2)}) copy-start(f32[64]{0:T(128)} %param.6) | copy-start | bytes 772
  13.1 87.5 %all-to-all-start = ((bf16[4,2,55296]{2,1,0:T(2,128)(2,1)}), bf16[4,2,55296]{2,1,0:T(2,128)(2,1)S(1)}, u32[]{:S(2)}, u32[]{:S(2)}) async-start(bf16[4,2,55296]{2,1,0:T(2,128)(2,1)} %reshape.20), calls=%async_computation | async-start | bytes 1769472 | tf_op jit(solution)/shard_map/all_to_all | solution.py:371
  18.3 149.0 %all-reduce.2.cloned.1.call-start = ((), (), s32[]{:S(2)}) async-start(), calls=%async_computation.1 | async-start | bytes 3538944 | tf_op jit(solution)/shard_map/psum | solution.py:387
  103.1 64.2 %copy-start.1 = (bf16[4,16,64,128]{3,2,1,0:T(8,128)(2,1)S(1)}, bf16[4,16,64,128]{3,2,1,0:T(8,128)(2,1)}, u32[]{:S(2)}) copy-start(bf16[4,16,64,128]{3,2,1,0:T(8,128)(2,1)} %get-tuple-element.12) | copy-start | bytes 3145732
  160.1 8.2 %copy-start.2 = (bf16[4,16,64,128]{3,2,1,0:T(8,128)(2,1)S(1)}, bf16[4,16,64,128]{3,2,1,0:T(8,128)(2,1)}, u32[]{:S(2)}) copy-start(bf16[4,16,64,128]{3,2,1,0:T(8,128)(2,1)} %shard_map.68) | copy-start | bytes 3145732
  167.3 1.9 %copy-start = (f32[27,64,256]{2,1,0:T(8,128)S(1)}, f32[27,64,256]{2,1,0:T(8,128)}, u32[]{:S(2)}) copy-start(f32[27,64,256]{2,1,0:T(8,128)} %all-reduce.2.cloned.1.call-done) | copy-start | bytes 5308420
Sparse Core Ops, SparseCore 0:
  100.7 66.5 all-reduce.1
where the time goes:
time: 178 us; the launch traced here: 177 us
  Pallas kernels  139 us (78%)
  between operations  14.1 us (8%)
  local copies, waits for them, and re-layouts  12.3 us (7%)
  waiting for transfers between devices  7.23 us (4%)
  starting transfers between devices  5.19 us (3%)
    pallas_call x2, Pallas kernels, call(): pl.pallas_call(functools.partial(kernel, peers), out_shape=outs, in_specs...  139 us
    unnamed x13, local copies, waits for them, and re-layouts  8.18 us
    psum x1, waiting for transfers between devices, on_device(): weight_grad = lax.psum(partial, 'space').reshape(taps, outs, chans)  7.21 us
    all_to_all x1, starting transfers between devices, on_device(): lax.all_to_all(pieces, 'chan', split_axis=0, concat_axis=0, tiled=True)  5.19 us
  transfers between devices with their start and end apart: 2, of which 1 were waited for; matrix products, arithmetic and copies ran while one was open for 2% of the time, Pallas kernels for 78%

commit v1 on v0

v1 whole, which is shorter than its diff:
```python
import functools
import math

import jax
import jax.numpy as jnp
from jax import lax
from jax.experimental import pallas as pl
from jax.experimental.pallas import tpu as pltpu
from jax.sharding import PartitionSpec as P

F32 = jnp.float32
BF16 = jnp.bfloat16
VMEM_LIMIT = 60 * 1024 * 1024


def shifted(rows, amount):
    size_z = rows.shape[1]
    lane = lax.broadcasted_iota(jnp.int32, rows.shape, 1)
    edge = 0 if amount == 1 else size_z - 1
    return jnp.where(lane == edge, 0.0, pltpu.roll(rows, amount % size_z, 1))


class Gather:
    def __init__(self, source, shape, planes, local_sem, send_sem, recv_sem, halo_send, halo_recv, peers, order):
        self.source, self.planes = source, planes
        self.local_sem, self.send_sem, self.recv_sem = local_sem, send_sem, recv_sem
        self.halo_send, self.halo_recv = halo_send, halo_recv
        self.size_x, self.size_y, self.part, self.size_z = shape
        self.peers = peers
        self.me = lax.axis_index("chan")
        self.slab = lax.axis_index("space")
        self.slabs = lax.axis_size("space")
        self.chans = self.part * peers
        self.has_lo, self.has_hi = self.slab > 0, self.slab < self.slabs - 1
        self.order = list(order)
        me = self.me
        if peers == 4:
            across = me // 2 * 2 + (1 - me % 2)
            along = (1 - me // 2) * 2 + me % 2
            self.owners = [me, across, along, 3 - me]
            self.near = [1, 2]
        else:
            self.owners = [(me + r) % peers for r in range(peers)]
            self.near = list(range(1, peers))

    def block(self, q, owner):
        rows = pl.ds(pl.multiple_of(q * self.chans + owner * self.part, self.part), self.part)
        return self.planes.at[rows, self.size_z : (self.size_y + 1) * self.size_z]

    def back(self, slot):
        return slot if self.peers == 4 else self.peers - slot

    def chan_copy(self, q, slot_held, toward, slot_there):
        return pltpu.make_async_remote_copy(
            src_ref=self.block(q, self.owners[slot_held]),
            dst_ref=self.block(q, self.owners[slot_held]),
            send_sem=self.send_sem.at[q, slot_there],
            recv_sem=self.recv_sem.at[q, slot_there],
            device_id=(self.me, self.slab) if toward is None else (self.owners[toward], self.slab),
            device_id_type=pl.DeviceIdType.MESH,
        )

    def arrived(self, q, slot):
        pltpu.make_async_remote_copy(
            src_ref=self.block(q, self.owners[slot]),
            dst_ref=self.block(q, self.owners[slot]),
            send_sem=self.send_sem.at[q, slot],
            recv_sem=self.recv_sem.at[q, slot],
            device_id=(self.owners[1], self.slab),
            device_id_type=pl.DeviceIdType.MESH,
        ).wait_recv()

    def halo_copy(self, slot, up):
        mine, theirs = (self.size_x, 0) if up else (1, self.size_x + 1)
        return pltpu.make_async_remote_copy(
            src_ref=self.block(mine, self.owners[slot]),
            dst_ref=self.block(theirs, self.owners[slot]),
            send_sem=self.halo_send.at[int(up), slot],
            recv_sem=self.halo_recv.at[int(up), slot],
            device_id=(self.me, self.slab + 1 if up else self.slab - 1),
            device_id_type=pl.DeviceIdType.MESH,
        )

    def halo_pass(self, q, slot):
        if q == self.size_x:

            @pl.when(self.has_hi)
            def _():
                self.halo_copy(slot, True).start()

        if q == 1:

            @pl.when(self.has_lo)
            def _():
                self.halo_copy(slot, False).start()

    def local_copy(self, q, y):
        rows = pl.ds(pl.multiple_of(q * self.chans + self.me * self.part, self.part), self.part)
        lanes = pl.ds(pl.multiple_of((y + 1) * self.size_z, self.size_z), self.size_z)
        return pltpu.make_async_copy(
            self.source.at[q - 1, y], self.planes.at[rows, lanes], self.local_sem.at[q]
        )

    def start_local(self):
        for q in self.order:

            def put(y, _, q=q):
                self.local_copy(q, y).start()
                return 0

            lax.fori_loop(0, self.size_y, put, 0)

    def wait_local(self, q):
        def done(y, _):
            self.local_copy(q, y).wait()
            return 0

        lax.fori_loop(0, self.size_y, done, 0)

    def clear(self):
        edge = jnp.zeros((self.planes.shape[0], self.size_z), BF16)
        self.planes[:, 0 : self.size_z] = edge
        self.planes[:, (self.size_y + 1) * self.size_z : (self.size_y + 2) * self.size_z] = edge
        cells = slice(self.size_z, (self.size_y + 1) * self.size_z)
        blank = jnp.zeros((self.chans, self.size_y * self.size_z), BF16)

        @pl.when(jnp.logical_not(self.has_lo))
        def _():
            self.planes[0 : self.chans, cells] = blank

        @pl.when(jnp.logical_not(self.has_hi))
        def _():
            self.planes[(self.size_x + 1) * self.chans : (self.size_x + 2) * self.chans, cells] = blank

    def send_own(self, stage):
        q = self.order[stage]
        for slot in self.near:
            self.chan_copy(q, 0, slot, self.back(slot)).start()
        self.halo_pass(q, 0)

    def relay(self, stage, q, slot):
        return self.peers == 4 and slot == (1 if stage % 2 else 2)

    def take_near(self, stage):
        q = self.order[stage]
        for slot in self.near:
            self.arrived(q, slot)
            if self.relay(stage, q, slot):
                self.chan_copy(q, slot, 3 - slot, 3).start()
            self.halo_pass(q, slot)
        if self.source is not None and stage + 2 < len(self.order):
            self.wait_local(self.order[stage + 2])
            self.send_own(stage + 2)

    def take_far(self, stage):
        q = self.order[stage]
        if self.peers == 4:
            self.arrived(q, 3)
            self.halo_pass(q, 3)

    def take_halo(self, up):
        @pl.when(self.has_lo if up else self.has_hi)
        def _():
            for slot in range(self.peers):
                mine, theirs = (self.size_x, 0) if up else (1, self.size_x + 1)
                pltpu.make_async_remote_copy(
                    src_ref=self.block(mine, self.owners[slot]),
                    dst_ref=self.block(theirs, self.owners[slot]),
                    send_sem=self.halo_send.at[int(up), slot],
                    recv_sem=self.halo_recv.at[int(up), slot],
                    device_id=(self.me, self.slab - 1 if up else self.slab + 1),
                    device_id_type=pl.DeviceIdType.MESH,
                ).wait_recv()

    def finish(self):
        for stage, q in enumerate(self.order):
            for slot in self.near:
                self.chan_copy(q, 0, slot, self.back(slot)).wait_send()
                if self.relay(stage, q, slot):
                    self.chan_copy(q, slot, 3 - slot, 3).wait_send()
        for up, there in ((True, self.has_hi), (False, self.has_lo)):

            @pl.when(there)
            def _(up=up):
                for slot in range(self.peers):
                    self.halo_copy(slot, up).wait_send()


def add_plane(planes, w_ref, acc, q, started, chans, size_y, size_z):
    size_x, rows, _ = acc.shape
    taps = [dx for dx in range(3) if 0 <= q - dx < size_x]
    first, last = taps[0], taps[-1] + 1
    count = 2

    def step(index, _):
        y = index * count
        total = None
        for dy in range(3):
            lanes = pl.ds(pl.multiple_of((y + dy) * size_z, size_z), count * size_z)
            part = jnp.dot(
                w_ref[first:last, dy].reshape((last - first) * rows, chans),
                planes[q * chans : (q + 1) * chans, lanes],
                preferred_element_type=F32,
            )
            total = part if total is None else total + part
        lanes = pl.ds(pl.multiple_of(y * size_z, size_z), count * size_z)
        for dx in taps:
            part = total[(dx - first) * rows : (dx - first + 1) * rows]
            if q - dx in started:
                acc[q - dx, :, lanes] += part
            else:
                acc[q - dx, :, lanes] = part
        return 0

    lax.fori_loop(0, size_y // count, step, 0)
    started.update(q - dx for dx in taps)


def tap_sum(acc, x, outs, lanes):
    return (
        acc[x, outs : 2 * outs, lanes]
        + shifted(acc[x, 0:outs, lanes], 1)
        + shifted(acc[x, 2 * outs : 3 * outs, lanes], -1)
    )


def tap_sum(acc, x, outs, lanes):
    return (
        acc[x, outs : 2 * outs, lanes]
        + shifted(acc[x, 0:outs, lanes], 1)
        + shifted(acc[x, 2 * outs : 3 * outs, lanes], -1)
    )


class Planes:
    def __init__(self, gather, w_ref, acc, finish_plane):
        self.gather, self.w_ref, self.acc, self.finish_plane = gather, w_ref, acc, finish_plane
        self.started, self.count = set(), {x: 3 for x in range(gather.size_x)}

    def add(self, q):
        g = self.gather
        add_plane(g.planes, self.w_ref, self.acc, q, self.started, g.chans, g.size_y, g.size_z)
        for dx in range(3):
            x = q - dx
            if x in self.count:
                self.count[x] -= 1
                if self.count[x] == 0:
                    self.finish_plane(x)


def plane_order(size_x):
    order = [1] + ([size_x] if size_x > 1 else []) + list(range(2, size_x))
    used = order[:-1] + [0, size_x + 1] + order[-1:]
    count, done = {x: 3 for x in range(size_x)}, []
    for q in used:
        for dx in range(3):
            if q - dx in count:
                count[q - dx] -= 1
                if count[q - dx] == 0:
                    done.append(q - dx + 1)
    return order, done


class Weights:
    def __init__(self, w_ref, blocks, got, turned, sems, gather):
        self.w_ref, self.blocks, self.got, self.turned = w_ref, blocks, got, turned
        self.local_sem, self.send_sem, self.recv_sem, self.pass_send, self.pass_recv = sems
        self.gather = gather
        self.peers, self.groups, self.outs, lanes = blocks.shape
        self.ins = gather.part
        self.each = lanes // self.ins
        self.half = self.groups // 2
        self.core = lax.rem(gather.slab, 2)
        self.partner = gather.slab + 1 - 2 * self.core

    def build(self):
        def step(k, _):
            taps = []
            for u in range(self.each):
                tap = jnp.minimum(k * self.each + u, 26)
                rows = pl.ds(pl.multiple_of(tap % 3 * self.outs, self.outs), self.outs)
                taps.append(self.w_ref[tap // 9, tap // 3 % 3, rows].astype(F32))
            for j in range(self.peers):
                part = [t[:, j * self.ins : (j + 1) * self.ins] for t in taps]
                self.blocks[j, k] = jnp.concatenate(part, axis=1).astype(BF16)
            return 0

        lax.fori_loop(0, self.groups, step, 0)

    def own(self):
        me = self.gather.me
        return pltpu.make_async_copy(self.blocks.at[me], self.got.at[me], self.local_sem)

    def copy(self, slot):
        g = self.gather
        rows = pl.ds(self.core * self.half, self.half)
        there = g.back(slot)
        return pltpu.make_async_remote_copy(
            src_ref=self.blocks.at[g.owners[slot], rows],
            dst_ref=self.got.at[g.me, rows],
            send_sem=self.send_sem.at[there],
            recv_sem=self.recv_sem.at[there],
            device_id=(g.owners[slot], g.slab),
            device_id_type=pl.DeviceIdType.MESH,
        )

    def arrival(self, slot, core, send_sem, recv_sem):
        g = self.gather
        rows = self.got.at[g.owners[slot], pl.ds(core * self.half, self.half)]
        return pltpu.make_async_remote_copy(
            src_ref=rows,
            dst_ref=rows,
            send_sem=send_sem.at[slot],
            recv_sem=recv_sem.at[slot],
            device_id=(g.me, self.partner),
            device_id_type=pl.DeviceIdType.MESH,
        )

    def send(self):
        self.own().start()
        for slot in range(1, self.peers):
            self.copy(slot).start()

    def hand_on(self):
        for slot in range(1, self.peers):
            self.arrival(slot, self.core, self.send_sem, self.recv_sem).wait_recv()
            self.arrival(slot, self.core, self.pass_send, self.pass_recv).start()

    def turn(self):
        self.own().wait()
        for slot in range(1, self.peers):
            self.arrival(slot, 1 - self.core, self.pass_send, self.pass_recv).wait_recv()

        def step(k, _):
            whole = jnp.concatenate([self.got[j, k] for j in range(self.peers)], axis=0)
            whole = whole.astype(F32).T.astype(BF16)
            for u in range(self.each):
                tap = 26 - (k * self.each + u)

                @pl.when(tap >= 0)
                def _():
                    at = jnp.maximum(tap, 0)
                    rows = pl.ds(pl.multiple_of(at % 3 * self.ins, self.ins), self.ins)
                    self.turned[at // 9, at // 3 % 3, rows] = whole[u * self.ins : (u + 1) * self.ins]

            return 0

        lax.fori_loop(0, self.groups, step, 0)

    def finish(self):
        for slot in range(1, self.peers):
            self.copy(slot).wait_send()
            self.arrival(slot, self.core, self.pass_send, self.pass_recv).wait_send()


class Reduce:
    def __init__(self, total, other, paired, mine, line, result, sems, slab, slabs, me):
        self.total, self.other, self.paired, self.mine = total, other, paired, mine
        self.line, self.result, self.me = line, result, me
        (
            self.pair_send,
            self.pair_recv,
            self.line_send,
            self.line_recv,
            self.cast_send,
            self.cast_recv,
            self.back_send,
            self.back_recv,
        ) = sems
        self.members, self.chunk, self.cols = line.shape
        self.half = self.members * self.chunk
        self.core, self.place = lax.rem(slab, 2), slab // 2
        self.partner = slab + 1 - 2 * self.core

    def rows(self, start):
        return pl.ds(pl.multiple_of(start * self.chunk, self.chunk), self.chunk)

    def member(self, r):
        return lax.rem(self.place + r, self.members)

    def remote(self, src, dst, send, recv, slab):
        return pltpu.make_async_remote_copy(
            src_ref=src,
            dst_ref=dst,
            send_sem=send,
            recv_sem=recv,
            device_id=(self.me, slab),
            device_id_type=pl.DeviceIdType.MESH,
        )

    def pair(self):
        return self.remote(self.other, self.paired, self.pair_send, self.pair_recv, self.partner)

    def along(self, r):
        return self.remote(
            self.mine.at[self.rows(self.member(r))],
            self.line.at[r],
            self.line_send.at[r],
            self.line_recv.at[r],
            self.member(r) * 2 + self.core,
        )

    def block(self, core, place):
        return self.result.at[self.rows(core * self.members + place)]

    def cast(self, r):
        own = self.block(self.core, self.place)
        slab = self.member(r) * 2 + self.core
        return self.remote(own, own, self.cast_send.at[r], self.cast_recv.at[r], slab)

    def came(self, r):
        block = self.block(self.core, self.member(self.members - r))
        return self.remote(block, block, self.cast_send.at[r], self.cast_recv.at[r], self.partner)

    def hand_back(self, r, core):
        block = self.block(core, self.member(self.members - r))
        return self.remote(block, block, self.back_send.at[r], self.back_recv.at[r], self.partner)

    def start(self):
        def step(k, _):
            rows = self.rows((1 - self.core) * self.members + k)
            self.other[self.rows(k)] = self.total[rows].astype(BF16)
            return 0

        lax.fori_loop(0, self.members, step, 0)
        self.pair().start()

    def second(self):
        self.pair().wait_recv()

        def step(k, _):
            rows = self.rows(self.core * self.members + k)
            both = self.total[rows] + self.paired[self.rows(k)].astype(F32)
            self.total[rows] = both
            self.mine[self.rows(k)] = both.astype(BF16)
            return 0

        lax.fori_loop(0, self.members, step, 0)
        for r in range(1, self.members):
            self.along(r).start()

    def third(self, scale):
        for r in range(1, self.members):
            self.along(r).wait_recv()
        rows = self.rows(self.core * self.members + self.place)
        whole = self.total[rows]
        for r in range(1, self.members):
            whole = whole + self.line[r].astype(F32)
        self.result[rows] = (whole * scale).astype(BF16)
        for r in range(1, self.members):
            self.cast(r).start()
        self.hand_back(0, self.core).start()

    def fourth(self):
        for r in range(1, self.members):
            self.came(r).wait_recv()
            self.hand_back(r, self.core).start()

    def last(self):
        for r in range(self.members):
            self.hand_back(r, 1 - self.core).wait_recv()

    def finish(self):
        self.pair().wait_send()
        for r in range(self.members):
            if r:
                self.along(r).wait_send()
                self.cast(r).wait_send()
            self.hand_back(r, self.core).wait_send()


def fused_kernel(
    peers, slabs, vol_ref, w_ref, bias_ref, cot_ref, out_ref, input_ref, weight_ref,
    planes, grads, acc, three, total, other, paired, mine, line, result, blocks, got, turned, local_sem, *sems
):
    size_x, size_y, outs, size_z = cot_ref.shape
    order, done = plane_order(size_x)
    vol = Gather(vol_ref, cot_ref.shape, planes, local_sem, *sems[0:4], peers, order)
    grad = Gather(None, cot_ref.shape, grads, None, *sems[4:8], peers, done)
    weights = Weights(w_ref, blocks, got, turned, sems[8:13], vol)
    reduce = Reduce(total, other, paired, mine, line, result, sems[13:21], vol.slab, slabs, vol.me)
    chans, cells = vol.chans, size_y * size_z

    vol.start_local()
    barrier = pltpu.get_barrier_semaphore()
    for slot in range(1, peers):
        device = (vol.owners[slot], vol.slab)
        pl.semaphore_signal(barrier, inc=1, device_id=device, device_id_type=pl.DeviceIdType.MESH)
    for r in range(1, slabs):
        device = (vol.me, lax.rem(vol.slab + r, slabs))
        pl.semaphore_signal(barrier, inc=1, device_id=device, device_id_type=pl.DeviceIdType.MESH)
    vol.clear()
    pl.semaphore_wait(barrier, peers - 1 + slabs - 1)
    for stage in range(min(2, size_x)):
        vol.wait_local(order[stage])
        vol.send_own(stage)
    grad.clear()
    total[...] = jnp.zeros_like(total)
    weights.build()
    bias = jnp.broadcast_to(bias_ref[...], (size_z, outs)).T
    mine_rows = pl.multiple_of(vol.me * outs, outs)

    def finish_forward(x):
        rows = pl.ds(pl.multiple_of((x + 1) * chans + mine_rows, outs), outs)

        def step(y, _):
            lanes = pl.ds(pl.multiple_of(y * size_z, size_z), size_z)
            pre = tap_sum(acc, x, outs, lanes) + bias
            sig = jax.nn.sigmoid(pre)
            out_ref[x, y] = (pre * sig).astype(BF16)
            held = (cot_ref[x, y].astype(F32) * sig * (1.0 + pre * (1.0 - sig))).astype(BF16)
            grads[rows, pl.ds(pl.multiple_of((y + 1) * size_z, size_z), size_z)] = held
            value = held.astype(F32)
            three[x, 0:outs, lanes] = shifted(value, -1).astype(BF16)
            three[x, outs : 2 * outs, lanes] = held
            three[x, 2 * outs : 3 * outs, lanes] = shifted(value, 1).astype(BF16)
            return 0

        lax.fori_loop(0, size_y, step, 0)
        grad.send_own(done.index(x + 1))

    def finish_input(x):
        def step(y, _):
            lanes = pl.ds(pl.multiple_of(y * size_z, size_z), size_z)
            input_ref[x, y] = tap_sum(acc, x, outs, lanes).astype(BF16)
            return 0

        lax.fori_loop(0, size_y, step, 0)

    forward = Planes(vol, w_ref, acc, finish_forward)
    stages = size_x
    for stage in range(stages):
        vol.take_near(stage)
        if stage == min(1, stages - 1):
            weights.send()
        if stage:
            vol.take_far(stage - 1)
            forward.add(order[stage - 1])
    vol.take_halo(True)
    forward.add(0)
    vol.take_halo(False)
    forward.add(size_x + 1)
    vol.take_far(stages - 1)
    forward.add(order[-1])
    weights.hand_on()

    def weight_grad(first, last):
        def step(x, _):
            for dy in range(3):
                cube = planes[pl.ds(pl.multiple_of(x * chans, chans), 3 * chans), dy * size_z : dy * size_z + cells]
                part = lax.dot_general(three[x], cube, (((1,), (1,)), ((), ())), preferred_element_type=F32)
                for dx in range(3):
                    at = (dx * 3 + dy) * 3 * outs
                    total[at : at + 3 * outs] += part[:, dx * chans : (dx + 1) * chans]
            return 0

        lax.fori_loop(first, last, step, 0)

    backward = Planes(grad, turned, acc, finish_input)
    grad.take_near(0)
    weight_grad(0, size_x // 2)
    if stages > 1:
        grad.take_near(1)
    weight_grad(size_x // 2, size_x)
    reduce.start()
    weights.turn()
    grad.take_far(0)
    later = [reduce.second, functools.partial(reduce.third, 1.0 / math.sqrt(size_x * cells * slabs)), reduce.fourth]
    for stage in range(2, stages + 1):
        backward.add(done[stage - 2])
        if later:
            later.pop(0)()
        if stage < stages:
            grad.take_near(stage)
        grad.take_far(stage - 1)
    grad.take_halo(True)
    backward.add(0)
    if later:
        later.pop(0)()
    grad.take_halo(False)
    backward.add(size_x + 1)
    while later:
        later.pop(0)()
    backward.add(done[-1])
    reduce.last()
    weight_ref[...] = result[0 : weight_ref.shape[0]].astype(F32)
    vol.finish()
    grad.finish()
    weights.finish()
    reduce.finish()


def on_device(volume, kernel, bias, cotangent):
    size_x, size_y, part, size_z = volume.shape
    taps, outs, chans = kernel.shape
    shape = jax.ShapeDtypeStruct
    flops = 2 * size_x * size_y * size_z * taps * outs * chans
    peers, slabs = lax.axis_size("chan"), lax.axis_size("space")
    each = max(1, size_z // part)
    groups = 2 * -(-taps // (2 * each))
    members = slabs // 2
    chunk = 16 * -(-taps * outs // (slabs * 16))
    whole = pl.BlockSpec(memory_space=pltpu.VMEM)
    args = (volume, kernel.reshape(3, 3, 3 * outs, chans), bias.reshape(1, outs), cotangent)
    planes = size_x + 2
    dma = pltpu.SemaphoreType.DMA
    sides = [dma((planes, peers)), dma((planes, peers)), dma((2, peers)), dma((2, peers))]
    output, input_grad, weight_grad = pl.pallas_call(
        functools.partial(fused_kernel, peers, slabs),
        out_shape=(
            shape(cotangent.shape, BF16),
            shape(volume.shape, BF16),
            shape((taps * outs, chans), F32),
        ),
        in_specs=[pl.BlockSpec(memory_space=pl.ANY)] + [whole] * 3,
        out_specs=(whole, whole, whole),
        scratch_shapes=[
            pltpu.VMEM((planes * chans, (size_y + 2) * size_z), BF16),
            pltpu.VMEM((planes * chans, (size_y + 2) * size_z), BF16),
            pltpu.VMEM((size_x, 3 * outs, size_y * size_z), F32),
            pltpu.VMEM((size_x, 3 * outs, size_y * size_z), BF16),
            pltpu.VMEM((slabs * chunk, chans), F32),
            pltpu.VMEM((members * chunk, chans), BF16),
            pltpu.VMEM((members * chunk, chans), BF16),
            pltpu.VMEM((members * chunk, chans), BF16),
            pltpu.VMEM((members, chunk, chans), BF16),
            pltpu.VMEM((slabs * chunk, chans), BF16),
            pltpu.VMEM((peers, groups, outs, each * part), BF16),
            pltpu.VMEM((peers, groups, outs, each * part), BF16),
            pltpu.VMEM((3, 3, 3 * part, chans), BF16),
            dma((planes,)),
            *sides,
            *sides,
            dma(()),
            dma((peers,)),
            dma((peers,)),
            dma((peers,)),
            dma((peers,)),
            dma(()),
            dma(()),
            *[dma((members,)) for _ in range(6)],
        ],
        compiler_params=pltpu.CompilerParams(vmem_limit_bytes=VMEM_LIMIT, collective_id=0, has_side_effects=True),
        cost_estimate=pl.CostEstimate(flops=3 * flops, bytes_accessed=8 * volume.size, transcendentals=0),
    )(*args)
    return output, input_grad, weight_grad.reshape(taps, outs, chans)


def solution(mesh):
    return jax.shard_map(
        on_device,
        mesh=mesh,
        in_specs=(
            P("space", None, "chan", None),
            P(None, "chan", None),
            P("chan"),
            P("space", None, "chan", None),
        ),
        out_specs=(
            P("space", None, "chan", None),
            P("space", None, "chan", None),
            P(None, "chan", None),
        ),
        check_vma=False,
    )
```

time: 178 us -> 135 us (0.76)
  between operations: 14.1 us -> 0.66 us
  Pallas kernels: 139 us -> 130 us
  local copies, waits for them, and re-layouts: 12.3 us -> 4.6 us
  waiting for transfers between devices: 7.23 us -> 0 us
  starting transfers between devices: 5.19 us -> 0 us
    pallas_call x2 -> x1, Pallas kernels: 139 us -> 130 us  [on_device(): pl.pallas_call(functools.partial(fused_kernel, peers, slabs), out_shape=(...]
    psum x1 -> x0, waiting for transfers between devices: 7.21 us -> none  [on_device(): weight_grad = lax.psum(partial, 'space').reshape(taps, outs, chans)]
    all_to_all x1 -> x0, starting transfers between devices: 5.19 us -> none  [on_device(): lax.all_to_all(pieces, 'chan', split_axis=0, concat_axis=0, tiled=True)]
    unnamed x13 -> x7, local copies, waits for them, and re-layouts: 8.18 us -> 4.6 us
    reshape x2 -> x0, local copies, waits for them, and re-layouts: 3.41 us -> none  [on_device(): pieces = kernel.reshape(taps, outs, peers, ins).transpose(2, 0, 1, 3)]
  transfers between devices with their start and end apart: 2 -> 0, of which waited for: 1 -> 0; matrix products, arithmetic and copies ran while one was open for 2% -> 0% of each run, Pallas kernels for 78% -> 0%
where the time goes in v1:
time: 135 us
  Pallas kernels  130 us (96%)
  local copies, waits for them, and re-layouts  4.6 us (3%)
    pallas_call x1, Pallas kernels, on_device(): pl.pallas_call(functools.partial(fused_kernel, peers, slabs), out_shape=(...  130 us
    unnamed x7, local copies, waits for them, and re-layouts  4.6 us

profile of v1, /device:TPU:0, one launch (start us, length us, event | category | flops | bytes accessed | tf_op | source)
XLA Modules:
  0.0 134.8 jit_solution(16357120934220963207)
XLA Ops:
  0.6 129.5 %shard_map.67 = (bf16[4,16,64,128]{3,2,1,0:T(8,128)(2,1)}, bf16[4,16,64,128]{3,2,1,0:T(8,128)(2,1)}, f32[1728,256]{1,0:T(8,128)}) custom-call(bf16[4,16,64,128]{3,2,1,0:T(8,128)(2,1)} %vol_ref.1, bf16[3,3,192,256]{3,2,1,0:T(8,128)(2,1)} %bitcast.4, f32[1,64]{1,0:T(1,128)} %bitcast.5, bf16[4,16,64,128]{3,2,1,0:T(8,128)(2,1)} %cot_ref.1), custom_call_target="tpu_custom_call" | custom-call | flops 21743271936 | bytes 4194304 | tf_op jit(solution)/shard_map/pallas_call | solution.py:608
  130.2 0.0 copy-start.1
  130.2 0.0 copy-start
  130.2 2.4 %copy.10 = bf16[4,16,64,128]{3,2,1,0:T(8,128)(2,1)} copy(bf16[4,16,64,128]{3,2,1,0:T(8,128)(2,1)} %get-tuple-element.12) | data formatting | bytes 2097152
  132.6 0.0 copy-done.1
  132.6 1.0 copy.11
  133.6 0.0 copy-done
  133.6 1.2 copy.12
Async XLA Ops:
  130.2 2.4 %copy-start.1 = (bf16[4,16,64,128]{3,2,1,0:T(8,128)(2,1)S(1)}, bf16[4,16,64,128]{3,2,1,0:T(8,128)(2,1)}, u32[]{:S(2)}) copy-start(bf16[4,16,64,128]{3,2,1,0:T(8,128)(2,1)} %get-tuple-element.13) | copy-start | bytes 3145732
  130.2 3.4 %copy-start = (f32[1728,256]{1,0:T(8,128)S(1)}, f32[1728,256]{1,0:T(8,128)}, u32[]{:S(2)}) copy-start(f32[1728,256]{1,0:T(8,128)} %get-tuple-element.8) | copy-start | bytes 5308420

commit v2 on v1

--- a/solution.py
+++ b/solution.py
@@ -43,29 +43,33 @@
             self.owners = [(me + r) % peers for r in range(peers)]
             self.near = list(range(1, peers))
 
-    def block(self, q, owner):
+    def block(self, q, owner, half=None):
         rows = pl.ds(pl.multiple_of(q * self.chans + owner * self.part, self.part), self.part)
-        return self.planes.at[rows, self.size_z : (self.size_y + 1) * self.size_z]
+        first, last = (0, 2) if half is None else (half, half + 1)
+        each = self.size_y * self.size_z // 2
+        return self.planes.at[rows, self.size_z + first * each : self.size_z + last * each]
 
     def back(self, slot):
         return slot if self.peers == 4 else self.peers - slot
 
-    def chan_copy(self, q, slot_held, toward, slot_there):
+    def chan_copy(self, q, slot_held, toward, slot_there, half):
+        block = self.block(q, self.owners[slot_held], half)
         return pltpu.make_async_remote_copy(
-            src_ref=self.block(q, self.owners[slot_held]),
-            dst_ref=self.block(q, self.owners[slot_held]),
-            send_sem=self.send_sem.at[q, slot_there],
-            recv_sem=self.recv_sem.at[q, slot_there],
-            device_id=(self.me, self.slab) if toward is None else (self.owners[toward], self.slab),
+            src_ref=block,
+            dst_ref=block,
+            send_sem=self.send_sem.at[q, slot_there, half],
+            recv_sem=self.recv_sem.at[q, slot_there, half],
+            device_id=(self.owners[toward], self.slab),
             device_id_type=pl.DeviceIdType.MESH,
         )
 
-    def arrived(self, q, slot):
+    def arrived(self, q, slot, half):
+        block = self.block(q, self.owners[slot], half)
         pltpu.make_async_remote_copy(
-            src_ref=self.block(q, self.owners[slot]),
-            dst_ref=self.block(q, self.owners[slot]),
-            send_sem=self.send_sem.at[q, slot],
-            recv_sem=self.recv_sem.at[q, slot],
+            src_ref=block,
+            dst_ref=block,
+            send_sem=self.send_sem.at[q, slot, half],
+            recv_sem=self.recv_sem.at[q, slot, half],
             device_id=(self.owners[1], self.slab),
             device_id_type=pl.DeviceIdType.MESH,
         ).wait_recv()
@@ -134,19 +138,22 @@
 
     def send_own(self, stage):
         q = self.order[stage]
-        for slot in self.near:
-            self.chan_copy(q, 0, slot, self.back(slot)).start()
+        for half in range(2):
+            for slot in self.near:
+                self.chan_copy(q, 0, slot, self.back(slot), half).start()
         self.halo_pass(q, 0)
 
-    def relay(self, stage, q, slot):
-        return self.peers == 4 and slot == (1 if stage % 2 else 2)
+    def relay(self, slot, half):
+        return self.peers == 4 and slot == half + 1
 
     def take_near(self, stage):
         q = self.order[stage]
+        for half in range(2):
+            for slot in self.near:
+                self.arrived(q, slot, half)
+                if self.relay(slot, half):
+                    self.chan_copy(q, slot, 3 - slot, 3, half).start()
         for slot in self.near:
-            self.arrived(q, slot)
-            if self.relay(stage, q, slot):
-                self.chan_copy(q, slot, 3 - slot, 3).start()
             self.halo_pass(q, slot)
         if self.source is not None and stage + 2 < len(self.order):
             self.wait_local(self.order[stage + 2])
@@ -155,7 +162,8 @@
     def take_far(self, stage):
         q = self.order[stage]
         if self.peers == 4:
-            self.arrived(q, 3)
+            for half in range(2):
+                self.arrived(q, 3, half)
             self.halo_pass(q, 3)
 
     def take_halo(self, up):
@@ -173,11 +181,12 @@
                 ).wait_recv()
 
     def finish(self):
-        for stage, q in enumerate(self.order):
-            for slot in self.near:
-                self.chan_copy(q, 0, slot, self.back(slot)).wait_send()
-                if self.relay(stage, q, slot):
-                    self.chan_copy(q, slot, 3 - slot, 3).wait_send()
+        for q in self.order:
+            for half in range(2):
+                for slot in self.near:
+                    self.chan_copy(q, 0, slot, self.back(slot), half).wait_send()
+                    if self.relay(slot, half):
+                        self.chan_copy(q, slot, 3 - slot, 3, half).wait_send()
         for up, there in ((True, self.has_hi), (False, self.has_lo)):
 
             @pl.when(there)
@@ -190,7 +199,7 @@
     size_x, rows, _ = acc.shape
     taps = [dx for dx in range(3) if 0 <= q - dx < size_x]
     first, last = taps[0], taps[-1] + 1
-    count = 2
+    count = 4 if size_y % 4 == 0 else 1
 
     def step(index, _):
         y = index * count
@@ -540,9 +549,9 @@
     forward.add(0)
     vol.take_halo(False)
     forward.add(size_x + 1)
+    weights.hand_on()
     vol.take_far(stages - 1)
     forward.add(order[-1])
-    weights.hand_on()
 
     def weight_grad(first, last):
         def step(x, _):
@@ -565,22 +574,23 @@
     reduce.start()
     weights.turn()
     grad.take_far(0)
-    later = [reduce.second, functools.partial(reduce.third, 1.0 / math.sqrt(size_x * cells * slabs)), reduce.fourth]
+    scale = 1.0 / math.sqrt(size_x * cells * slabs)
+    later = [reduce.second, functools.partial(reduce.third, scale), reduce.fourth]
     for stage in range(2, stages + 1):
         backward.add(done[stage - 2])
-        if later:
-            later.pop(0)()
         if stage < stages:
             grad.take_near(stage)
-        grad.take_far(stage - 1)
+            if len(later) > 1:
+                later.pop(0)()
+            grad.take_far(stage - 1)
     grad.take_halo(True)
     backward.add(0)
-    if later:
+    while len(later) > 1:
         later.pop(0)()
     grad.take_halo(False)
     backward.add(size_x + 1)
-    while later:
-        later.pop(0)()
+    later.pop(0)()
+    grad.take_far(stages - 1)
     backward.add(done[-1])
     reduce.last()
     weight_ref[...] = result[0 : weight_ref.shape[0]].astype(F32)
@@ -604,7 +614,7 @@
     args = (volume, kernel.reshape(3, 3, 3 * outs, chans), bias.reshape(1, outs), cotangent)
     planes = size_x + 2
     dma = pltpu.SemaphoreType.DMA
-    sides = [dma((planes, peers)), dma((planes, peers)), dma((2, peers)), dma((2, peers))]
+    sides = [dma((planes, peers, 2)), dma((planes, peers, 2)), dma((2, peers)), dma((2, peers))]
     output, input_grad, weight_grad = pl.pallas_call(
         functools.partial(fused_kernel, peers, slabs),
         out_shape=(

time: 135 us -> 123 us (0.911)
  Pallas kernels: 130 us -> 117 us
    pallas_call x1, Pallas kernels: 130 us -> 117 us  [on_device(): pl.pallas_call(functools.partial(fused_kernel, peers, slabs), out_shape=(...]
where the time goes in v2:
time: 123 us; the launch traced here: 122 us
  Pallas kernels  117 us (95%)
  local copies, waits for them, and re-layouts  4.6 us (4%)
    pallas_call x1, Pallas kernels, on_device(): pl.pallas_call(functools.partial(fused_kernel, peers, slabs), out_shape=(...  117 us
    unnamed x7, local copies, waits for them, and re-layouts  4.6 us

profile of v2, /device:TPU:0, one launch (start us, length us, event | category | flops | bytes accessed | tf_op | source)
XLA Modules:
  0.0 122.1 jit_solution(4772545965361688162)
XLA Ops:
  0.6 116.8 %shard_map.67 = (bf16[4,16,64,128]{3,2,1,0:T(8,128)(2,1)}, bf16[4,16,64,128]{3,2,1,0:T(8,128)(2,1)}, f32[1728,256]{1,0:T(8,128)}) custom-call(bf16[4,16,64,128]{3,2,1,0:T(8,128)(2,1)} %vol_ref.1, bf16[3,3,192,256]{3,2,1,0:T(8,128)(2,1)} %bitcast.4, f32[1,64]{1,0:T(1,128)} %bitcast.5, bf16[4,16,64,128]{3,2,1,0:T(8,128)(2,1)} %cot_ref.1), custom_call_target="tpu_custom_call" | custom-call | flops 21743271936 | bytes 4194304 | tf_op jit(solution)/shard_map/pallas_call | solution.py:618
  117.5 0.0 copy-start.1
  117.5 0.0 copy-start
  117.5 2.4 %copy.10 = bf16[4,16,64,128]{3,2,1,0:T(8,128)(2,1)} copy(bf16[4,16,64,128]{3,2,1,0:T(8,128)(2,1)} %get-tuple-element.12) | data formatting | bytes 2097152
  119.9 0.0 copy-done.1
  119.9 1.0 copy.11
  120.9 0.0 copy-done
  120.9 1.2 copy.12
Async XLA Ops:
  117.5 2.4 %copy-start.1 = (bf16[4,16,64,128]{3,2,1,0:T(8,128)(2,1)S(1)}, bf16[4,16,64,128]{3,2,1,0:T(8,128)(2,1)}, u32[]{:S(2)}) copy-start(bf16[4,16,64,128]{3,2,1,0:T(8,128)(2,1)} %get-tuple-element.13) | copy-start | bytes 3145732
  117.5 3.4 %copy-start = (f32[1728,256]{1,0:T(8,128)S(1)}, f32[1728,256]{1,0:T(8,128)}, u32[]{:S(2)}) copy-start(f32[1728,256]{1,0:T(8,128)} %get-tuple-element.8) | copy-start | bytes 5308420
